TPU v7x, 32 devices: a whole 2x2x4 slice. The times are simulated.
32 devices in a mesh: ctx: 16 (over z, y, x), section: 2 (over core).
Axes of the slice: x: 2, y: 2, z: 4, core: 2. Of those that a mesh axis runs over, the one named last changes fastest.
Arguments:
- layer_inputs: bfloat16 [2, 4096, 1536], P('section', 'ctx'), may hold values from -6 to 6
- conv_weight: bfloat16 [2, 3, 1536, 768], P('section', None, 'ctx'), may hold values from -0.09375 to 0.09375
- mix_weight: bfloat16 [2, 768, 1536], P('section', 'ctx'), may hold values from -0.21875 to 0.21875
- bn_scale: float32 [2, 1536], P('section'), may hold values from 0.5 to 2
- bn_shift: float32 [2, 1536], P('section'), may hold values from -4 to 4
- cotangent: bfloat16 [4096, 1536], P('ctx'), may hold values from -6 to 6
Outputs:
- input_grads: bfloat16 [2, 4096, 1536], P('section', 'ctx')
All inputs are finite; a program needn't handle non-finite values.
Results may differ from a plain program's by a relative error of at most 0.0053.
Values may be sent and summed in bfloat16 or wider, within the bound.
A program may use at most 64 MiB of HBM per device.

v0:
```python
import jax
import jax.numpy as jnp
from jax import lax
from jax.sharding import PartitionSpec as P


def extended(cells, sides, width):
    for axis, dim in sides:
        count = lax.axis_size(axis)
        ends = count - 1
        head = lax.slice_in_dim(cells, 0, width, axis=dim)
        tail = lax.slice_in_dim(cells, cells.shape[dim] - width, cells.shape[dim], axis=dim)
        cells = jnp.concatenate(
            [
                lax.ppermute(tail, axis, [(i, (i + 1) % count) for i in range(ends)]),
                cells,
                lax.ppermute(head, axis, [((i + 1) % count, i) for i in range(ends)]),
            ],
            axis=dim,
        )
    return cells


def shifted(block, axis, distance):
    devices = range(lax.axis_size(axis))
    route = [(i - distance, i) for i in devices if i - distance in devices]
    return lax.ppermute(block, axis, route)


def gelu_parts(value):
    cdf = 0.5 * (1.0 + lax.erf(value * 0.7071067811865476))
    dens = jnp.exp(-0.5 * value * value) * 0.3989422804014327
    return (value * cdf, cdf + value * dens)


def shards(layer_inputs, conv_weight, mix_weight, bn_scale, bn_shift, cotangent):
    sections = lax.axis_size("section")
    level = lax.axis_index("section")
    widest = 2 ** (sections - 1)
    conv_full, mix_full = (
        lax.all_gather(conv_weight, "ctx", axis=2, tiled=True),
        lax.all_gather(mix_weight, "ctx", axis=1, tiled=True),
    )
    conv_full = conv_full[0]
    mix_full = mix_full[0]
    rows = cotangent.shape[0]
    inner = mix_full.shape[0]
    spacing = jnp.left_shift(jnp.int32(1), level)
    pre = layer_inputs[0].astype(jnp.float32) * bn_scale[0] + bn_shift[0]
    act, slope_pre = gelu_parts(pre)
    hidden = act.astype(jnp.bfloat16)
    padded = extended(hidden, (("ctx", 0),), widest)
    conv = jnp.zeros((rows, inner), jnp.float32)
    for k in range(3):
        window = lax.dynamic_slice_in_dim(padded, widest + (k - 1) * spacing, rows, 0)
        conv = conv + jnp.dot(window, conv_full[k], preferred_element_type=jnp.float32)
    _, slope_conv = gelu_parts(conv)
    factor = slope_pre * bn_scale[0]

    def make_dconv(grad):
        back = jnp.einsum("pc,hc->ph", grad, mix_full, preferred_element_type=jnp.float32)
        return (back * slope_conv).astype(jnp.bfloat16)

    def skip_dconv(grad):
        return jnp.zeros((rows, inner), jnp.bfloat16)

    def finish(grad, dpad, starts):
        dhidden = jnp.zeros((rows, conv_full.shape[1]), jnp.float32)
        for k in range(3):
            window = lax.dynamic_slice_in_dim(dpad, starts[k], rows, 0)
            dhidden = dhidden + jnp.einsum(
                "ph,ch->pc", window, conv_full[k], preferred_element_type=jnp.float32
            )
        return (grad.astype(jnp.float32) + dhidden * factor).astype(jnp.bfloat16)

    mine = jnp.zeros_like(cotangent)

    def turn(step, carry):
        grad, mine = carry
        active = level == sections - 1 - step
        dconv = lax.cond(active, make_dconv, skip_dconv, grad)
        dpad = extended(dconv, (("ctx", 0),), widest)
        starts = [widest + (1 - k) * spacing for k in range(3)]
        result = lax.cond(active, lambda g: finish(g, dpad, starts), lambda g: g, grad)
        mine = jnp.where(active, result, mine)
        grad = shifted(result, "section", -1)
        return (grad, mine)

    grad, mine = lax.fori_loop(0, sections, turn, (cotangent, mine))
    return mine[None]


def solution(mesh):
    return jax.shard_map(
        shards,
        mesh=mesh,
        in_specs=(
            P("section", "ctx", None),
            P("section", None, "ctx", None),
            P("section", "ctx", None),
            P("section", None),
            P("section", None),
            P("ctx", None),
        ),
        out_specs=P("section", "ctx", None),
        check_vma=False,
    )
```

profile of v0, /device:TPU:0, one launch (start us, length us, event | category | flops | bytes accessed | tf_op | source)
XLA Modules:
  0.0 225.2 jit_solution(1895826705466310313)
XLA Ops:
  6.5 0.0 copy-start.2
  6.5 0.0 copy-start.3
  6.5 0.0 all-gather.5.cloned.1.call-start
  6.5 0.7 all-gather.5.cloned.1.call-update
  7.3 0.0 all-gather.3.cloned.1.call-start
  7.3 0.7 all-gather.3.cloned.1.call-update
  8.0 0.0 copy-done.2
  8.1 0.0 copy-done.3
  8.1 0.0 copy-done.1
  8.1 2.0 fusion.28
  10.1 4.9 %collective-permute-start.3 = (bf16[2,1536]{1,0:T(2,128)(2,1)S(1)}, bf16[2,1536]{1,0:T(2,128)(2,1)S(1)}, u32[]{:S(2)}, u32[]{:S(2)}) collective-permute-start(bf16[2,1536]{1,0:T(2,128)(2,1)S(1)} %get-tuple-element.330), channel_id=1, source_target_pairs={{0,2},{2,4},{4,6},{6,8},{8,10},{10,12},{12,14},{14,16},{16,18},{18... | collective-permute-start | bytes 18440 | tf_op jit(solution)/shard_map/ppermute | solution.py:15
  15.0 1.3 collective-permute-start.4
  16.3 0.0 collective-permute-done.3
  16.3 4.2 %collective-permute-done.4 = bf16[2,1536]{1,0:T(2,128)(2,1)S(1)} collective-permute-done((bf16[2,1536]{1,0:T(2,128)(2,1)S(1)}, bf16[2,1536]{1,0:T(2,128)(2,1)S(1)}, u32[]{:S(2)}, u32[]{:S(2)}) %collective-permute-start.4) | collective-permute-done | bytes 6176 | tf_op jit(solution)/shard_map/ppermute | solution.py:17
  20.5 0.2 pad_maximum_fusion.1
  20.7 92.7 %all-gather.5.cloned.1.call-done = bf16[1,3,1536,768]{3,2,1,0:T(8,128)(2,1)} async-done(((bf16[1,3,96,768]{3,2,1,0:T(8,128)(2,1)}), bf16[1,3,1536,768]{3,2,1,0:T(8,128)(2,1)}) %all-gather.5.cloned.1.call-update) | async-done | bytes 7077904 | tf_op jit(solution)/shard_map/all_gather | solution.py:41
  113.4 2.4 %fusion.15 = f32[256,768]{1,0:T(8,128)S(1)} fusion(bf16[1,3,1536,768]{3,2,1,0:T(8,128)(2,1)} %all-gather.5.cloned.1.call-done, bf16[260,1536]{1,0:T(8,128)(2,1)S(1)} %pad_maximum_fusion.1, s32[]{:T(128)S(6)} %select_n.33), kind=kOutput, calls=%fused_computation.22 | convolution fusion | flops 603979776 | bytes 3932164 | tf_op jit(solution)/shard_map/dot_general | solution.py:56
  115.8 2.7 %fusion.16 = f32[256,768]{1,0:T(8,128)S(1)} fusion(bf16[1,3,1536,768]{3,2,1,0:T(8,128)(2,1)} %all-gather.5.cloned.1.call-done, bf16[1,256,1536]{2,1,0:T(8,128)(2,1)S(1)} %copy-done.1, f32[1536]{0:T(1024)S(1)} %reduce.1, f32[1536]{0:T(1024)S(1)} %reduce), kind=kOutput, calls=%fused_computation.24 | convolution fusion | flops 607125504 | bytes 3944448 | tf_op jit(solution)/shard_map/dot_general | solution.py:56
  118.5 0.0 copy-start
  118.5 3.6 %fusion.43 = f32[256,768]{1,0:T(8,128)} fusion(f32[256,768]{1,0:T(8,128)S(1)} %fusion.15, f32[256,768]{1,0:T(8,128)S(1)} %fusion.16, bf16[1,3,1536,768]{3,2,1,0:T(8,128)(2,1)} %all-gather.5.cloned.1.call-done, bf16[260,1536]{1,0:T(8,128)(2,1)S(1)} %pad_maximum_fusion.1, s32[]{:T(128)S(6)} %select_n.32), kind=kOutput, calls=%fused_computation.56 | convolution fusion | flops 605945856 | bytes 5505028 | tf_op jit(solution)/shard_map/dot_general | solution.py:56
  122.1 54.7 %all-gather.3.cloned.1.call-done = bf16[1,768,1536]{2,1,0:T(8,128)(2,1)} async-done(((bf16[1,48,1536]{2,1,0:T(8,128)(2,1)}), bf16[1,768,1536]{2,1,0:T(8,128)(2,1)}) %all-gather.3.cloned.1.call-update) | async-done | bytes 2359312 | tf_op jit(solution)/shard_map/all_gather | solution.py:42
  176.8 0.0 copy-done
  176.8 41.6 %while.21 = (s32[]{:T(128)}, bf16[256,1536]{1,0:T(8,128)(2,1)S(1)}, bf16[256,1536]{1,0:T(8,128)(2,1)}, s32[]{:T(128)}, bf16[768,1536]{1,0:T(8,128)(2,1)}, /*inde...) while((s32[]{:T(128)}, bf16[256,1536]{1,0:T(8,128)(2,1)S(1)}, ...), condition=%wide.region_5.6_spmd.clone, body=%wide.region_0.5_spmd.clone.sunk | while | flops 2420656128 | bytes 29934024 | solution.py:89
  176.8 0.1 copy.15
  176.8 0.1 conditional.6
  176.9 1.3 collective-permute-start
  178.2 4.5 %collective-permute-start.1 = (bf16[2,768]{1,0:T(2,128)(2,1)S(1)}, bf16[2,768]{1,0:T(2,128)(2,1)S(1)}, u32[]{:S(2)}, u32[]{:S(2)}) collective-permute-start(bf16[2,768]{1,0:T(2,128)(2,1)S(1)} %get-tuple-element.396), channel_id=1, source_target_pairs={{0,2},{2,4},{4,6},{6,8},{8,10},{10,12},{12,14},{14,16},{16,18},{18... | collective-permute-start | bytes 9224 | tf_op jit(solution)/shard_map/while/body/eval_jaxpr/ppermute | solution.py:15
  182.8 0.0 collective-permute-done
  182.8 1.3 collective-permute-done.1
  184.1 0.1 pad_maximum_fusion.3
  184.2 1.3 collective-permute-start.2
  185.5 1.0 select_select_fusion.2
  186.5 9.2 %collective-permute-done.2 = bf16[256,1536]{1,0:T(8,128)(2,1)S(1)} collective-permute-done((bf16[256,1536]{1,0:T(8,128)(2,1)S(1)}, bf16[256,1536]{1,0:T(8,128)(2,1)S(1)}, u32[]{:S(2)}, u32[]{:S(2)}) %collective-permute-start.2) | collective-permute-done | bytes 786464 | tf_op jit(solution)/shard_map/while/body/eval_jaxpr/ppermute | solution.py:27
  195.7 0.1 copy.15
  195.7 2.7 %conditional.6 = (bf16[256,768]{1,0:T(8,128)(2,1)S(1)}) conditional(s32[]{:T(128)} %convert_element_type.108, () %tuple.68, (bf16[256,1536]{1,0:T(8,128)(2,1)S(1)}, bf16[768,1536]{1,0:T(8,128)(2,1)}, f32[256,768]{1,0:T(8,128)}) %tuple.69), branch_computations={%region_1.0_spmd, %region_2.0_spmd} | conditional | flops 604372992 | bytes 4325384 | solution.py:81
  195.8 2.6 %fusion = bf16[256,768]{1,0:T(8,128)(2,1)S(1)} fusion(f32[256,768]{1,0:T(8,128)} %get-tuple-element.252, bf16[256,1536]{1,0:T(8,128)(2,1)S(1)} %get-tuple-element.250, bf16[768,1536]{1,0:T(8,128)(2,1)} %get-tuple-element.251), kind=kOutput, calls=%fused_computation.1 | convolution fusion | flops 604372992 | bytes 4325376 | tf_op jit(solution)/shard_map/while/body/eval_jaxpr/cond/branch_1_fun/pc,hc->ph/dot_general | solution.py:61
  198.4 1.3 collective-permute-start
  199.7 4.9 %collective-permute-start.1 = (bf16[2,768]{1,0:T(2,128)(2,1)S(1)}, bf16[2,768]{1,0:T(2,128)(2,1)S(1)}, u32[]{:S(2)}, u32[]{:S(2)}) collective-permute-start(bf16[2,768]{1,0:T(2,128)(2,1)S(1)} %get-tuple-element.396), channel_id=1, source_target_pairs={{0,2},{2,4},{4,6},{6,8},{8,10},{10,12},{12,14},{14,16},{16,18},{18... | collective-permute-start | bytes 9224 | tf_op jit(solution)/shard_map/while/body/eval_jaxpr/ppermute | solution.py:15
  204.6 0.0 collective-permute-done
  204.7 1.3 collective-permute-done.1
  205.9 0.1 pad_maximum_fusion.3
  206.0 8.2 %conditional.7 = (bf16[256,1536]{1,0:T(8,128)(2,1)S(1)}) conditional(s32[]{:T(128)} %convert_element_type.108, bf16[256,1536]{1,0:T(8,128)(2,1)S(1)} %copy.15, (bf16[256,1536]{1,0:T(8,128)(2,1)S(1)}, s32[]{:T(128)}, bf16[260,768]{1,0:T(8,128)(2,1)S(1)}, bf16[3,1536,768]{2,1,0:T(8,128)(2,1)}, bf16[256,768]{1,0:T(8,128)(2,1)S(1)}, /*index=5*/s32[]{:T(128)}, ...), branch_computations={%region_3.0_spmd, %region_4.0_spmd} | conditional | flops 1814298624 | bytes 17694804 | solution.py:84
  206.1 2.5 %fusion.6 = f32[256,1536]{1,0:T(8,128)S(1)} fusion(bf16[3,1536,768]{2,1,0:T(8,128)(2,1)} %get-tuple-element.256, bf16[260,768]{1,0:T(8,128)(2,1)S(1)} %get-tuple-element.254, s32[]{:T(128)S(6)} %select_n.26), kind=kOutput, calls=%fused_computation.9 | convolution fusion | flops 603979776 | bytes 4325380 | tf_op jit(solution)/shard_map/while/body/eval_jaxpr/cond/branch_1_fun/ph,ch->pc/dot_general | solution.py:71
  208.6 2.5 %convolution_add_fusion.1 = f32[256,1536]{1,0:T(8,128)S(1)} fusion(f32[256,1536]{1,0:T(8,128)S(1)} %fusion.6, bf16[256,768]{1,0:T(8,128)(2,1)S(1)} %get-tuple-element.257, bf16[3,1536,768]{2,1,0:T(8,128)(2,1)} %get-tuple-element.256), kind=kOutput, calls=%fused_computation.5 | convolution fusion | flops 604372992 | bytes 5898240 | tf_op jit(solution)/shard_map/while/body/eval_jaxpr/cond/branch_1_fun/ph,ch->pc/dot_general | solution.py:71
  211.1 3.1 %fusion.3 = bf16[256,1536]{1,0:T(8,128)(2,1)S(1)} fusion(f32[256,1536]{1,0:T(8,128)} %get-tuple-element.259, f32[256,1536]{1,0:T(8,128)S(1)} %convolution_add_fusion.1, bf16[3,1536,768]{2,1,0:T(8,128)(2,1)} %get-tuple-element.256, bf16[256,1536]{1,0:T(8,128)(2,1)S(1)} %get-tuple-element.253, bf16[260,768]{1,0:T(8,128)(2,1)S(1)} %get-tuple-element.254, ...), kind=kOutput, calls=%fused_computation.6 | convolution fusion | flops 605945856 | bytes 7471108 | tf_op jit(solution)/shard_map/while/body/eval_jaxpr/cond/branch_1_fun/ph,ch->pc/dot_general | solution.py:71
  214.2 1.3 collective-permute-start.2
  215.5 2.1 select_select_fusion.2
  217.6 0.8 collective-permute-done.2
  (9 shorter events, 0.1 us)
Async XLA Ops:
  6.5 1.5 copy-start.2
  6.5 1.5 copy-start.3
  6.5 1.6 copy-start.1
  6.5 106.8 %all-gather.5.cloned.1.call-start = ((), (), s32[]{:S(2)}) async-start(), calls=%async_computation.1 | async-start | bytes 7520256 | tf_op jit(solution)/shard_map/all_gather | solution.py:41
  7.3 169.5 %all-gather.3.cloned.1.call-start = ((), (), s32[]{:S(2)}) async-start(), calls=%async_computation | async-start | bytes 2506752 | tf_op jit(solution)/shard_map/all_gather | solution.py:42
  10.1 6.2 %collective-permute-start.3 = (bf16[2,1536]{1,0:T(2,128)(2,1)S(1)}, bf16[2,1536]{1,0:T(2,128)(2,1)S(1)}, u32[]{:S(2)}, u32[]{:S(2)}) collective-permute-start(bf16[2,1536]{1,0:T(2,128)(2,1)S(1)} %get-tuple-element.330), channel_id=1, source_target_pairs={{0,2},{2,4},{4,6},{6,8},{8,10},{10,12},{12,14},{14,16},{16,18},{18... | collective-permute-start | bytes 18440 | tf_op jit(solution)/shard_map/ppermute | solution.py:15
  15.0 5.5 %collective-permute-start.4 = (bf16[2,1536]{1,0:T(2,128)(2,1)S(1)}, bf16[2,1536]{1,0:T(2,128)(2,1)S(1)}, u32[]{:S(2)}, u32[]{:S(2)}) collective-permute-start(bf16[2,1536]{1,0:T(2,128)(2,1)S(1)} %get-tuple-element.331), channel_id=1, source_target_pairs={{2,0},{4,2},{6,4},{8,6},{10,8},{12,10},{14,12},{16,14},{18,16},{20... | collective-permute-start | bytes 18440 | tf_op jit(solution)/shard_map/ppermute | solution.py:17
  118.5 58.3 %copy-start = (bf16[256,1536]{1,0:T(8,128)(2,1)S(1)}, bf16[256,1536]{1,0:T(8,128)(2,1)}, u32[]{:S(2)}) copy-start(bf16[256,1536]{1,0:T(8,128)(2,1)} %param.17) | copy-start | bytes 2359300
  176.9 5.9 %collective-permute-start = (bf16[2,768]{1,0:T(2,128)(2,1)S(1)}, bf16[2,768]{1,0:T(2,128)(2,1)S(1)}, u32[]{:S(2)}, u32[]{:S(2)}) collective-permute-start(bf16[2,768]{1,0:T(2,128)(2,1)S(1)} %get-tuple-element.395), channel_id=1, source_target_pairs={{2,0},{4,2},{6,4},{8,6},{10,8},{12,10},{14,12},{16,14},{18,16},{20... | collective-permute-start | bytes 9224 | tf_op jit(solution)/shard_map/while/body/eval_jaxpr/ppermute | solution.py:17
  178.2 5.9 %collective-permute-start.1 = (bf16[2,768]{1,0:T(2,128)(2,1)S(1)}, bf16[2,768]{1,0:T(2,128)(2,1)S(1)}, u32[]{:S(2)}, u32[]{:S(2)}) collective-permute-start(bf16[2,768]{1,0:T(2,128)(2,1)S(1)} %get-tuple-element.396), channel_id=1, source_target_pairs={{0,2},{2,4},{4,6},{6,8},{8,10},{10,12},{12,14},{14,16},{16,18},{18... | collective-permute-start | bytes 9224 | tf_op jit(solution)/shard_map/while/body/eval_jaxpr/ppermute | solution.py:15
  184.2 11.5 %collective-permute-start.2 = (bf16[256,1536]{1,0:T(8,128)(2,1)S(1)}, bf16[256,1536]{1,0:T(8,128)(2,1)S(1)}, u32[]{:S(2)}, u32[]{:S(2)}) collective-permute-start(bf16[256,1536]{1,0:T(8,128)(2,1)S(1)} %get-tuple-element.434), channel_id=1, source_target_pairs={{1,0},{3,2},{5,4},{7,6},{9,8},{11,10},{13,12},{15,14},{17,16},{19,... | collective-permute-start | bytes 2359304 | tf_op jit(solution)/shard_map/while/body/eval_jaxpr/ppermute | solution.py:27
  198.4 6.2 %collective-permute-start = (bf16[2,768]{1,0:T(2,128)(2,1)S(1)}, bf16[2,768]{1,0:T(2,128)(2,1)S(1)}, u32[]{:S(2)}, u32[]{:S(2)}) collective-permute-start(bf16[2,768]{1,0:T(2,128)(2,1)S(1)} %get-tuple-element.395), channel_id=1, source_target_pairs={{2,0},{4,2},{6,4},{8,6},{10,8},{12,10},{14,12},{16,14},{18,16},{20... | collective-permute-start | bytes 9224 | tf_op jit(solution)/shard_map/while/body/eval_jaxpr/ppermute | solution.py:17
  199.7 6.2 %collective-permute-start.1 = (bf16[2,768]{1,0:T(2,128)(2,1)S(1)}, bf16[2,768]{1,0:T(2,128)(2,1)S(1)}, u32[]{:S(2)}, u32[]{:S(2)}) collective-permute-start(bf16[2,768]{1,0:T(2,128)(2,1)S(1)} %get-tuple-element.396), channel_id=1, source_target_pairs={{0,2},{2,4},{4,6},{6,8},{8,10},{10,12},{12,14},{14,16},{16,18},{18... | collective-permute-start | bytes 9224 | tf_op jit(solution)/shard_map/while/body/eval_jaxpr/ppermute | solution.py:15
  214.2 4.2 %collective-permute-start.2 = (bf16[256,1536]{1,0:T(8,128)(2,1)S(1)}, bf16[256,1536]{1,0:T(8,128)(2,1)S(1)}, u32[]{:S(2)}, u32[]{:S(2)}) collective-permute-start(bf16[256,1536]{1,0:T(8,128)(2,1)S(1)} %get-tuple-element.434), channel_id=1, source_target_pairs={{1,0},{3,2},{5,4},{7,6},{9,8},{11,10},{13,12},{15,14},{17,16},{19,... | collective-permute-start | bytes 2359304 | tf_op jit(solution)/shard_map/while/body/eval_jaxpr/ppermute | solution.py:27
Sparse Core Ops, SparseCore 0:
  10.0 103.3 all-gather.4
  116.2 60.5 all-gather.2
where the time goes:
time: 230 us; the launch traced here: 225 us
  waiting for transfers between devices  166 us (72%)
  starting transfers between devices  20.8 us (9%)
  matrix products  19.4 us (8%)
  between operations  13.5 us (6%)
  other arithmetic  5.51 us (2%)
    all_gather x1, waiting for transfers between devices, shards(): lax.all_gather(conv_weight, 'ctx', axis=2, tiled=True)  92.7 us
    all_gather x1, waiting for transfers between devices, shards(): lax.all_gather(mix_weight, 'ctx', axis=1, tiled=True)  54.7 us
    ppermute x3, starting transfers between devices, extended(): lax.ppermute(tail, axis, [(i, (i + 1) % count) for i in range(ends)])  14.3 us
    ppermute x2, waiting for transfers between devices, shifted(): return lax.ppermute(block, axis, route)  9.99 us
    dot_general x3, matrix products, shards(): jnp.dot(window, conv_full[k], preferred_element_type=jnp.float32)  8.68 us
    dot_general x3, matrix products, finish(): jnp.einsum('ph,ch->pc', window, conv_full[k], preferred_element_type=jnp....  8.11 us
  transfers between devices with their start and end apart: 10, of which 7 were waited for; matrix products, arithmetic and copies ran while one was open for 6% of the time, Pallas kernels for 0%

commit v1 on v0

--- a/solution.py
+++ b/solution.py
@@ -1,7 +1,204 @@
+import functools
 import jax
 import jax.numpy as jnp
 from jax import lax
+from jax.experimental import pallas as pl
+from jax.experimental.pallas import tpu as pltpu
 from jax.sharding import PartitionSpec as P
+
+MESH = pl.DeviceIdType.MESH
+HOPS = sorted(((t, ry, rx) for t in range(4) for ry in range(2) for rx in range(2)), key=sum)
+
+
+def place():
+    i = lax.axis_index("ctx")
+    return i // 4, (i // 2) % 2, i % 2
+
+
+def at(z, y, x):
+    return {"ctx": z * 4 + y * 2 + x}
+
+
+def greet():
+    z, y, x = place()
+    barrier = pltpu.get_barrier_semaphore()
+
+    def hello(device):
+        pl.semaphore_signal(barrier, inc=1, device_id=device, device_id_type=MESH)
+
+    hello(at(z, y, 1 - x))
+    hello(at(z, 1 - y, x))
+
+    @pl.when(z > 0)
+    def _():
+        hello(at(z - 1, y, x))
+
+    @pl.when(z < 3)
+    def _():
+        hello(at(z + 1, y, x))
+
+    ends = (z == 0).astype(jnp.int32) + (z == 3).astype(jnp.int32)
+    pl.semaphore_wait(barrier, 4 - ends)
+
+
+class Gather:
+    def __init__(self, conv, mix, conv_full, mix_full, send_sem, recv_sem):
+        self.conv, self.mix, self.conv_full, self.mix_full = conv, mix, conv_full, mix_full
+        self.send_sem, self.recv_sem = send_sem, recv_sem
+        depth, inner, wide = conv.shape[2], mix.shape[1], mix.shape[2]
+        third = inner // 3
+        self.depth, self.inner = depth, inner
+        self.parts = (
+            ("xzy", (0, 0, depth), (0, 0, wide), third),
+            ("yzx", (1, 0, depth), (third, 0, wide), third),
+            ("zxy", (2, 0, depth // 2), (2 * third, 0, wide // 2), third),
+            ("zyx", (2, depth // 2, depth // 2), (2 * third, wide // 2, wide // 2), third),
+        )
+
+    def own(self, part):
+        _, (tap, row, rows), (mrow, col, cols), third = self.parts[part]
+        return (
+            self.conv.at[0, tap, pl.ds(row, rows), :],
+            self.mix.at[0, pl.ds(mrow, third), pl.ds(col, cols)],
+        )
+
+    def full(self, part, source):
+        _, (tap, row, rows), (mrow, col, cols), third = self.parts[part]
+        return (
+            self.conv_full.at[tap, pl.ds(pl.multiple_of(source * self.depth + row, 16), rows), :],
+            self.mix_full.at[pl.ds(pl.multiple_of(source * self.inner + mrow, 16), third), pl.ds(col, cols)],
+        )
+
+    def copies(self, part, source, mine, lane, device):
+        here = self.own(part) if mine else self.full(part, source)
+        there = self.full(part, source)
+        return [
+            pltpu.make_async_remote_copy(
+                src_ref=here[m],
+                dst_ref=there[m],
+                send_sem=self.send_sem.at[part, source, lane, m],
+                recv_sem=self.recv_sem.at[part, source, m],
+                device_id=device,
+                device_id_type=MESH,
+            )
+            for m in range(2)
+        ]
+
+    def visit(self, t, ry, rx, part, sign, act):
+        z, y, x = place()
+        source = (z + sign * t) * 4 + (1 - y if ry else y) * 2 + (1 - x if rx else x)
+        mine = not (t or ry or rx)
+        differs = {"x": rx, "y": ry, "z": t}
+        order = self.parts[part][0]
+        for n in (2, 1, 0):
+            axis = order[n]
+            if any(differs[later] for later in order[n + 1:]):
+                continue
+            if axis == "x" and not rx:
+                act(self.copies(part, source, mine, 0, at(z, y, 1 - x)))
+            if axis == "y" and not ry:
+                act(self.copies(part, source, mine, 1, at(z, 1 - y, x)))
+            if axis == "z":
+                if t:
+                    lane = 2 + (1 + sign) // 2
+
+                    @pl.when((z - sign >= 0) & (z - sign < 4))
+                    def _():
+                        act(self.copies(part, source, mine, lane, at(z - sign, y, x)))
+                else:
+                    for lane, step in ((2, 1), (3, -1)):
+
+                        @pl.when((z + step >= 0) & (z + step < 4))
+                        def _():
+                            act(self.copies(part, source, mine, lane, at(z + step, y, x)))
+
+    def each(self, t, body):
+        if t == 0:
+            body(0)
+        else:
+            z = place()[0]
+
+            def side(b, c):
+                sign = 1 - 2 * b
+
+                @pl.when((z + sign * t >= 0) & (z + sign * t < 4))
+                def _():
+                    body(sign)
+
+                return c
+
+            lax.fori_loop(0, 2, side, 0)
+
+    def arrive(self, t, ry, rx, part, sign):
+        z, y, x = place()
+        source = (z + sign * t) * 4 + (1 - y if ry else y) * 2 + (1 - x if rx else x)
+        for copy in self.copies(part, source, False, 0, at(z, y, 1 - x)):
+            copy.wait_recv()
+
+    def hop(self, t, ry, rx):
+        def body(sign):
+            for part in range(4):
+                if t or ry or rx:
+                    self.arrive(t, ry, rx, part, sign)
+                self.visit(t, ry, rx, part, sign, lambda cs: [c.start() for c in cs])
+
+        self.each(t, body)
+
+    def drain(self):
+        for t, ry, rx in HOPS:
+
+            def body(sign):
+                for part in range(4):
+                    self.visit(t, ry, rx, part, sign, lambda cs: [c.wait_send() for c in cs])
+
+            self.each(t, body)
+
+
+def gather_kernel(conv, mix, conv_full, mix_full, send_sem, recv_sem, own_sem):
+    greet()
+    gather = Gather(conv, mix, conv_full, mix_full, send_sem, recv_sem)
+    gather.hop(0, 0, 0)
+    z, y, x = place()
+    me = z * 4 + y * 2 + x
+    local = [
+        pltpu.make_async_copy(
+            conv.at[0],
+            conv_full.at[:, pl.ds(pl.multiple_of(me * gather.depth, 16), gather.depth), :],
+            own_sem.at[0],
+        ),
+        pltpu.make_async_copy(
+            mix.at[0],
+            mix_full.at[pl.ds(pl.multiple_of(me * gather.inner, 16), gather.inner), :],
+            own_sem.at[1],
+        ),
+    ]
+    for copy in local:
+        copy.start()
+    for t, ry, rx in HOPS[1:]:
+        gather.hop(t, ry, rx)
+    for copy in local:
+        copy.wait()
+    gather.drain()
+
+
+def gathered(conv, mix):
+    count = lax.axis_size("ctx")
+    any_space = pl.BlockSpec(memory_space=pl.ANY)
+    return pl.pallas_call(
+        gather_kernel,
+        out_shape=(
+            jax.ShapeDtypeStruct((3, count * conv.shape[2], conv.shape[3]), conv.dtype),
+            jax.ShapeDtypeStruct((count * mix.shape[1], mix.shape[2]), mix.dtype),
+        ),
+        in_specs=[any_space] * 2,
+        out_specs=(any_space, any_space),
+        scratch_shapes=[
+            pltpu.SemaphoreType.DMA((4, 16, 4, 2)),
+            pltpu.SemaphoreType.DMA((4, 16, 2)),
+            pltpu.SemaphoreType.DMA((2,)),
+        ],
+        compiler_params=pltpu.CompilerParams(collective_id=0, has_side_effects=True),
+    )(conv, mix)
 
 
 def extended(cells, sides, width):
@@ -37,12 +234,11 @@
     sections = lax.axis_size("section")
     level = lax.axis_index("section")
     widest = 2 ** (sections - 1)
-    conv_full, mix_full = (
-        lax.all_gather(conv_weight, "ctx", axis=2, tiled=True),
-        lax.all_gather(mix_weight, "ctx", axis=1, tiled=True),
-    )
-    conv_full = conv_full[0]
-    mix_full = mix_full[0]
+    if lax.axis_size("ctx") == 16:
+        conv_full, mix_full = gathered(conv_weight, mix_weight)
+    else:
+        conv_full = lax.all_gather(conv_weight, "ctx", axis=2, tiled=True)[0]
+        mix_full = lax.all_gather(mix_weight, "ctx", axis=1, tiled=True)[0]
     rows = cotangent.shape[0]
     inner = mix_full.shape[0]
     spacing = jnp.left_shift(jnp.int32(1), level)

time: 230 us -> 145 us (0.63)
  the two profiles are of different devices: /device:TPU:0 before, /device:TPU:9 now
where the time goes in v1:
time: 145 us; the launch traced here: 144 us
  Pallas kernels  71.1 us (49%)
  starting transfers between devices  38.7 us (27%)
  matrix products  19.5 us (13%)
  waiting for transfers between devices  7.83 us (5%)
  other arithmetic  5.53 us (4%)
    pallas_call x1, Pallas kernels, gathered(): pl.pallas_call(gather_kernel, out_shape=(jax.ShapeDtypeStruct((3, count *...  71.1 us
    ppermute x2, starting transfers between devices, shifted(): return lax.ppermute(block, axis, route)  15.6 us
    ppermute x3, starting transfers between devices, extended(): lax.ppermute(head, axis, [((i + 1) % count, i) for i in range(ends)])  14.7 us
    dot_general x3, matrix products, shards(): jnp.dot(window, conv_full[k], preferred_element_type=jnp.float32)  8.73 us
    ppermute x3, starting transfers between devices, extended(): lax.ppermute(tail, axis, [(i, (i + 1) % count) for i in range(ends)])  8.4 us
    dot_general x3, matrix products, finish(): jnp.einsum('ph,ch->pc', window, conv_full[k], preferred_element_type=jnp....  8.13 us
    ppermute x3, waiting for transfers between devices, extended(): lax.ppermute(tail, axis, [(i, (i + 1) % count) for i in range(ends)])  6.96 us
    select_n x2, other arithmetic, turn(): mine = jnp.where(active, result, mine)  3.08 us
  transfers between devices with their start and end apart: 8, of which 3 were waited for; matrix products, arithmetic and copies ran while one was open for 4% of the time, Pallas kernels for 49%

profile of v1, /device:TPU:9, one launch (start us, length us, event | category | flops | bytes accessed | tf_op | source)
XLA Modules:
  0.0 144.3 jit_solution(18301128575573553682)
XLA Ops:
  0.0 0.0 copy-start.2
  0.0 0.0 copy-start.3
  0.0 0.0 copy-start.1
  0.0 0.7 copy-done.2
  0.7 0.0 copy-done.3
  0.8 0.4 copy-done.1
  1.2 2.0 %fusion.34 = (f32[256,1536]{1,0:T(8,128)}, bf16[256,1536]{1,0:T(8,128)(2,1)S(1)}) fusion(bf16[1,256,1536]{2,1,0:T(8,128)(2,1)S(1)} %copy-done.1, f32[1536]{0:T(1024)S(1)} %reduce.1, f32[1536]{0:T(1024)S(1)} %reduce), kind=kLoop, calls=%fused_computation.42 | loop fusion | flops 5505024 | bytes 3158016 | tf_op jit(solution)/shard_map/mul | solution.py:254
  3.2 3.1 %collective-permute-start.3 = (bf16[2,1536]{1,0:T(2,128)(2,1)S(1)}, bf16[2,1536]{1,0:T(2,128)(2,1)S(1)}, u32[]{:S(2)}, u32[]{:S(2)}) collective-permute-start(bf16[2,1536]{1,0:T(2,128)(2,1)S(1)} %get-tuple-element.334), channel_id=1, source_target_pairs={{0,2},{2,4},{4,6},{6,8},{8,10},{10,12},{12,14},{14,16},{16,18},{18... | collective-permute-start | bytes 18440 | tf_op jit(solution)/shard_map/ppermute | solution.py:212
  6.3 4.0 %collective-permute-start.4 = (bf16[2,1536]{1,0:T(2,128)(2,1)S(1)}, bf16[2,1536]{1,0:T(2,128)(2,1)S(1)}, u32[]{:S(2)}, u32[]{:S(2)}) collective-permute-start(bf16[2,1536]{1,0:T(2,128)(2,1)S(1)} %get-tuple-element.335), channel_id=1, source_target_pairs={{2,0},{4,2},{6,4},{8,6},{10,8},{12,10},{14,12},{16,14},{18,16},{20... | collective-permute-start | bytes 18440 | tf_op jit(solution)/shard_map/ppermute | solution.py:214
  10.3 71.1 %shard_map.64 = (bf16[3,1536,768]{2,1,0:T(8,128)(2,1)}, bf16[768,1536]{1,0:T(8,128)(2,1)}) custom-call(bf16[1,3,96,768]{3,2,1,0:T(8,128)(2,1)} %conv.1, bf16[1,48,1536]{2,1,0:T(8,128)(2,1)} %mix.1), custom_call_target="tpu_custom_call" | custom-call | tf_op jit(solution)/shard_map/pallas_call | solution.py:187
  81.4 2.7 %fusion.17 = f32[256,768]{1,0:T(8,128)S(1)} fusion(bf16[3,1536,768]{2,1,0:T(8,128)(2,1)} %get-tuple-element.408, bf16[1,256,1536]{2,1,0:T(8,128)(2,1)S(1)} %copy-done.1, f32[1536]{0:T(1024)S(1)} %reduce.1, f32[1536]{0:T(1024)S(1)} %reduce), kind=kOutput, calls=%fused_computation.23 | convolution fusion | flops 607125504 | bytes 3944448 | tf_op jit(solution)/shard_map/dot_general | solution.py:252
  84.1 0.0 collective-permute-done.3
  84.1 0.0 collective-permute-done.4
  84.1 0.2 pad_maximum_fusion.1
  84.3 2.5 %fusion.15 = f32[256,768]{1,0:T(8,128)S(1)} fusion(bf16[3,1536,768]{2,1,0:T(8,128)(2,1)} %get-tuple-element.408, bf16[260,1536]{1,0:T(8,128)(2,1)S(1)} %pad_maximum_fusion.1, s32[]{:T(128)S(6)} %select_n.33), kind=kOutput, calls=%fused_computation.21 | convolution fusion | flops 603979776 | bytes 3932164 | tf_op jit(solution)/shard_map/dot_general | solution.py:252
  86.8 0.0 copy-start
  86.8 3.6 %fusion.53 = f32[256,768]{1,0:T(8,128)} fusion(f32[256,768]{1,0:T(8,128)S(1)} %fusion.15, f32[256,768]{1,0:T(8,128)S(1)} %fusion.17, bf16[3,1536,768]{2,1,0:T(8,128)(2,1)} %get-tuple-element.408, bf16[260,1536]{1,0:T(8,128)(2,1)S(1)} %pad_maximum_fusion.1, s32[]{:T(128)S(6)} %select_n.32), kind=kOutput, calls=%fused_computation.59 | convolution fusion | flops 605945856 | bytes 5505028 | tf_op jit(solution)/shard_map/dot_general | solution.py:252
  90.4 0.0 copy-done
  90.4 53.9 %while.21 = (s32[]{:T(128)}, bf16[256,1536]{1,0:T(8,128)(2,1)S(1)}, bf16[256,1536]{1,0:T(8,128)(2,1)}, s32[]{:T(128)}, bf16[768,1536]{1,0:T(8,128)(2,1)}, /*inde...) while((s32[]{:T(128)}, bf16[256,1536]{1,0:T(8,128)(2,1)S(1)}, ...), condition=%wide.region_5.6_spmd.clone, body=%wide.region_0.5_spmd.clone.sunk | while | flops 2420656128 | bytes 29934024 | solution.py:285
  90.4 0.1 copy.15
  90.5 2.7 %conditional.6 = (bf16[256,768]{1,0:T(8,128)(2,1)S(1)}) conditional(s32[]{:T(128)} %convert_element_type.108, () %tuple.68, (bf16[256,1536]{1,0:T(8,128)(2,1)S(1)}, bf16[768,1536]{1,0:T(8,128)(2,1)}, f32[256,768]{1,0:T(8,128)}) %tuple.69), branch_computations={%region_1.0_spmd, %region_2.0_spmd} | conditional | flops 604372992 | bytes 4325384 | solution.py:277
  90.5 2.6 %fusion = bf16[256,768]{1,0:T(8,128)(2,1)S(1)} fusion(f32[256,768]{1,0:T(8,128)} %get-tuple-element.252, bf16[256,1536]{1,0:T(8,128)(2,1)S(1)} %get-tuple-element.250, bf16[768,1536]{1,0:T(8,128)(2,1)} %get-tuple-element.251), kind=kOutput, calls=%fused_computation.1 | convolution fusion | flops 604372992 | bytes 4325376 | tf_op jit(solution)/shard_map/while/body/eval_jaxpr/cond/branch_1_fun/pc,hc->ph/dot_general | solution.py:257
  93.2 8.8 %collective-permute-start = (bf16[2,768]{1,0:T(2,128)(2,1)S(1)}, bf16[2,768]{1,0:T(2,128)(2,1)S(1)}, u32[]{:S(2)}, u32[]{:S(2)}) collective-permute-start(bf16[2,768]{1,0:T(2,128)(2,1)S(1)} %get-tuple-element.399), channel_id=1, source_target_pairs={{2,0},{4,2},{6,4},{8,6},{10,8},{12,10},{14,12},{16,14},{18,16},{20... | collective-permute-start | bytes 9224 | tf_op jit(solution)/shard_map/while/body/eval_jaxpr/ppermute | solution.py:214
  102.0 1.9 %collective-permute-start.1 = (bf16[2,768]{1,0:T(2,128)(2,1)S(1)}, bf16[2,768]{1,0:T(2,128)(2,1)S(1)}, u32[]{:S(2)}, u32[]{:S(2)}) collective-permute-start(bf16[2,768]{1,0:T(2,128)(2,1)S(1)} %get-tuple-element.400), channel_id=1, source_target_pairs={{0,2},{2,4},{4,6},{6,8},{8,10},{10,12},{12,14},{14,16},{16,18},{18... | collective-permute-start | bytes 9224 | tf_op jit(solution)/shard_map/while/body/eval_jaxpr/ppermute | solution.py:212
  103.9 0.0 collective-permute-done
  103.9 4.2 %collective-permute-done.1 = bf16[2,768]{1,0:T(2,128)(2,1)S(1)} collective-permute-done((bf16[2,768]{1,0:T(2,128)(2,1)S(1)}, bf16[2,768]{1,0:T(2,128)(2,1)S(1)}, u32[]{:S(2)}, u32[]{:S(2)}) %collective-permute-start.1) | collective-permute-done | bytes 3104 | tf_op jit(solution)/shard_map/while/body/eval_jaxpr/ppermute | solution.py:212
  108.1 0.1 pad_maximum_fusion.3
  108.3 8.2 %conditional.7 = (bf16[256,1536]{1,0:T(8,128)(2,1)S(1)}) conditional(s32[]{:T(128)} %convert_element_type.108, bf16[256,1536]{1,0:T(8,128)(2,1)S(1)} %copy.15, (bf16[256,1536]{1,0:T(8,128)(2,1)S(1)}, s32[]{:T(128)}, bf16[260,768]{1,0:T(8,128)(2,1)S(1)}, bf16[3,1536,768]{2,1,0:T(8,128)(2,1)}, bf16[256,768]{1,0:T(8,128)(2,1)S(1)}, /*index=5*/s32[]{:T(128)}, ...), branch_computations={%region_3.0_spmd, %region_4.0_spmd} | conditional | flops 1814298624 | bytes 17694804 | solution.py:280
  108.3 2.5 %fusion.6 = f32[256,1536]{1,0:T(8,128)S(1)} fusion(bf16[3,1536,768]{2,1,0:T(8,128)(2,1)} %get-tuple-element.256, bf16[260,768]{1,0:T(8,128)(2,1)S(1)} %get-tuple-element.254, s32[]{:T(128)S(6)} %select_n.26), kind=kOutput, calls=%fused_computation.9 | convolution fusion | flops 603979776 | bytes 4325380 | tf_op jit(solution)/shard_map/while/body/eval_jaxpr/cond/branch_1_fun/ph,ch->pc/dot_general | solution.py:267
  110.8 2.5 %convolution_add_fusion.1 = f32[256,1536]{1,0:T(8,128)S(1)} fusion(f32[256,1536]{1,0:T(8,128)S(1)} %fusion.6, bf16[256,768]{1,0:T(8,128)(2,1)S(1)} %get-tuple-element.257, bf16[3,1536,768]{2,1,0:T(8,128)(2,1)} %get-tuple-element.256), kind=kOutput, calls=%fused_computation.5 | convolution fusion | flops 604372992 | bytes 5898240 | tf_op jit(solution)/shard_map/while/body/eval_jaxpr/cond/branch_1_fun/ph,ch->pc/dot_general | solution.py:267
  113.3 3.1 %fusion.3 = bf16[256,1536]{1,0:T(8,128)(2,1)S(1)} fusion(f32[256,1536]{1,0:T(8,128)} %get-tuple-element.259, f32[256,1536]{1,0:T(8,128)S(1)} %convolution_add_fusion.1, bf16[3,1536,768]{2,1,0:T(8,128)(2,1)} %get-tuple-element.256, bf16[256,1536]{1,0:T(8,128)(2,1)S(1)} %get-tuple-element.253, bf16[260,768]{1,0:T(8,128)(2,1)S(1)} %get-tuple-element.254, ...), kind=kOutput, calls=%fused_computation.6 | convolution fusion | flops 605945856 | bytes 7471108 | tf_op jit(solution)/shard_map/while/body/eval_jaxpr/cond/branch_1_fun/ph,ch->pc/dot_general | solution.py:267
  116.4 1.3 collective-permute-start.2
  117.8 1.0 select_select_fusion.2
  118.8 0.9 collective-permute-done.2
  119.6 0.1 copy.15
  119.7 0.1 conditional.6
  119.8 1.9 %collective-permute-start = (bf16[2,768]{1,0:T(2,128)(2,1)S(1)}, bf16[2,768]{1,0:T(2,128)(2,1)S(1)}, u32[]{:S(2)}, u32[]{:S(2)}) collective-permute-start(bf16[2,768]{1,0:T(2,128)(2,1)S(1)} %get-tuple-element.399), channel_id=1, source_target_pairs={{2,0},{4,2},{6,4},{8,6},{10,8},{12,10},{14,12},{16,14},{18,16},{20... | collective-permute-start | bytes 9224 | tf_op jit(solution)/shard_map/while/body/eval_jaxpr/ppermute | solution.py:214
  121.7 3.4 %collective-permute-start.1 = (bf16[2,768]{1,0:T(2,128)(2,1)S(1)}, bf16[2,768]{1,0:T(2,128)(2,1)S(1)}, u32[]{:S(2)}, u32[]{:S(2)}) collective-permute-start(bf16[2,768]{1,0:T(2,128)(2,1)S(1)} %get-tuple-element.400), channel_id=1, source_target_pairs={{0,2},{2,4},{4,6},{6,8},{8,10},{10,12},{12,14},{14,16},{16,18},{18... | collective-permute-start | bytes 9224 | tf_op jit(solution)/shard_map/while/body/eval_jaxpr/ppermute | solution.py:212
  125.1 0.0 collective-permute-done
  125.1 2.8 %collective-permute-done.1 = bf16[2,768]{1,0:T(2,128)(2,1)S(1)} collective-permute-done((bf16[2,768]{1,0:T(2,128)(2,1)S(1)}, bf16[2,768]{1,0:T(2,128)(2,1)S(1)}, u32[]{:S(2)}, u32[]{:S(2)}) %collective-permute-start.1) | collective-permute-done | bytes 3104 | tf_op jit(solution)/shard_map/while/body/eval_jaxpr/ppermute | solution.py:212
  127.8 0.1 pad_maximum_fusion.3
  127.9 14.3 %collective-permute-start.2 = (bf16[256,1536]{1,0:T(8,128)(2,1)S(1)}, bf16[256,1536]{1,0:T(8,128)(2,1)S(1)}, u32[]{:S(2)}, u32[]{:S(2)}) collective-permute-start(bf16[256,1536]{1,0:T(8,128)(2,1)S(1)} %get-tuple-element.438), channel_id=1, source_target_pairs={{1,0},{3,2},{5,4},{7,6},{9,8},{11,10},{13,12},{15,14},{17,16},{19,... | collective-permute-start | bytes 2359304 | tf_op jit(solution)/shard_map/while/body/eval_jaxpr/ppermute | solution.py:224
  142.2 2.1 %select_select_fusion.2 = bf16[256,1536]{1,0:T(8,128)(2,1)} fusion(bf16[256,1536]{1,0:T(8,128)(2,1)S(1)} %get-tuple-element.438, bf16[256,1536]{1,0:T(8,128)(2,1)} %get-tuple-element.415, pred[]{:T(512)S(6)} %compare.3, pred[]{:T(512)S(6)} %eq.11), kind=kLoop, calls=%fused_computation.18.clone.1 | loop fusion | flops 786432 | bytes 2359298 | tf_op jit(solution)/shard_map/while/body/eval_jaxpr/jit(_where)/select_n | solution.py:281
  144.3 0.0 collective-permute-done.2
  (8 shorter events, 0.1 us)
Async XLA Ops:
  0.0 0.7 copy-start.2
  0.0 0.7 copy-start.3
  0.0 1.2 copy-start.1
  3.2 80.9 %collective-permute-start.3 = (bf16[2,1536]{1,0:T(2,128)(2,1)S(1)}, bf16[2,1536]{1,0:T(2,128)(2,1)S(1)}, u32[]{:S(2)}, u32[]{:S(2)}) collective-permute-start(bf16[2,1536]{1,0:T(2,128)(2,1)S(1)} %get-tuple-element.334), channel_id=1, source_target_pairs={{0,2},{2,4},{4,6},{6,8},{8,10},{10,12},{12,14},{14,16},{16,18},{18... | collective-permute-start | bytes 18440 | tf_op jit(solution)/shard_map/ppermute | solution.py:212
  6.3 77.8 %collective-permute-start.4 = (bf16[2,1536]{1,0:T(2,128)(2,1)S(1)}, bf16[2,1536]{1,0:T(2,128)(2,1)S(1)}, u32[]{:S(2)}, u32[]{:S(2)}) collective-permute-start(bf16[2,1536]{1,0:T(2,128)(2,1)S(1)} %get-tuple-element.335), channel_id=1, source_target_pairs={{2,0},{4,2},{6,4},{8,6},{10,8},{12,10},{14,12},{16,14},{18,16},{20... | collective-permute-start | bytes 18440 | tf_op jit(solution)/shard_map/ppermute | solution.py:214
  86.8 3.6 %copy-start = (bf16[256,1536]{1,0:T(8,128)(2,1)S(1)}, bf16[256,1536]{1,0:T(8,128)(2,1)}, u32[]{:S(2)}) copy-start(bf16[256,1536]{1,0:T(8,128)(2,1)} %param.17) | copy-start | bytes 2359300
  93.2 10.8 %collective-permute-start = (bf16[2,768]{1,0:T(2,128)(2,1)S(1)}, bf16[2,768]{1,0:T(2,128)(2,1)S(1)}, u32[]{:S(2)}, u32[]{:S(2)}) collective-permute-start(bf16[2,768]{1,0:T(2,128)(2,1)S(1)} %get-tuple-element.399), channel_id=1, source_target_pairs={{2,0},{4,2},{6,4},{8,6},{10,8},{12,10},{14,12},{16,14},{18,16},{20... | collective-permute-start | bytes 9224 | tf_op jit(solution)/shard_map/while/body/eval_jaxpr/ppermute | solution.py:214
  102.0 6.1 %collective-permute-start.1 = (bf16[2,768]{1,0:T(2,128)(2,1)S(1)}, bf16[2,768]{1,0:T(2,128)(2,1)S(1)}, u32[]{:S(2)}, u32[]{:S(2)}) collective-permute-start(bf16[2,768]{1,0:T(2,128)(2,1)S(1)} %get-tuple-element.400), channel_id=1, source_target_pairs={{0,2},{2,4},{4,6},{6,8},{8,10},{10,12},{12,14},{14,16},{16,18},{18... | collective-permute-start | bytes 9224 | tf_op jit(solution)/shard_map/while/body/eval_jaxpr/ppermute | solution.py:212
  116.4 3.2 %collective-permute-start.2 = (bf16[256,1536]{1,0:T(8,128)(2,1)S(1)}, bf16[256,1536]{1,0:T(8,128)(2,1)S(1)}, u32[]{:S(2)}, u32[]{:S(2)}) collective-permute-start(bf16[256,1536]{1,0:T(8,128)(2,1)S(1)} %get-tuple-element.438), channel_id=1, source_target_pairs={{1,0},{3,2},{5,4},{7,6},{9,8},{11,10},{13,12},{15,14},{17,16},{19,... | collective-permute-start | bytes 2359304 | tf_op jit(solution)/shard_map/while/body/eval_jaxpr/ppermute | solution.py:224
  119.8 5.3 %collective-permute-start = (bf16[2,768]{1,0:T(2,128)(2,1)S(1)}, bf16[2,768]{1,0:T(2,128)(2,1)S(1)}, u32[]{:S(2)}, u32[]{:S(2)}) collective-permute-start(bf16[2,768]{1,0:T(2,128)(2,1)S(1)} %get-tuple-element.399), channel_id=1, source_target_pairs={{2,0},{4,2},{6,4},{8,6},{10,8},{12,10},{14,12},{16,14},{18,16},{20... | collective-permute-start | bytes 9224 | tf_op jit(solution)/shard_map/while/body/eval_jaxpr/ppermute | solution.py:214
  121.7 6.1 %collective-permute-start.1 = (bf16[2,768]{1,0:T(2,128)(2,1)S(1)}, bf16[2,768]{1,0:T(2,128)(2,1)S(1)}, u32[]{:S(2)}, u32[]{:S(2)}) collective-permute-start(bf16[2,768]{1,0:T(2,128)(2,1)S(1)} %get-tuple-element.400), channel_id=1, source_target_pairs={{0,2},{2,4},{4,6},{6,8},{8,10},{10,12},{12,14},{14,16},{16,18},{18... | collective-permute-start | bytes 9224 | tf_op jit(solution)/shard_map/while/body/eval_jaxpr/ppermute | solution.py:212
  127.9 16.4 %collective-permute-start.2 = (bf16[256,1536]{1,0:T(8,128)(2,1)S(1)}, bf16[256,1536]{1,0:T(8,128)(2,1)S(1)}, u32[]{:S(2)}, u32[]{:S(2)}) collective-permute-start(bf16[256,1536]{1,0:T(8,128)(2,1)S(1)} %get-tuple-element.438), channel_id=1, source_target_pairs={{1,0},{3,2},{5,4},{7,6},{9,8},{11,10},{13,12},{15,14},{17,16},{19,... | collective-permute-start | bytes 2359304 | tf_op jit(solution)/shard_map/while/body/eval_jaxpr/ppermute | solution.py:224

commit v2 on v1

--- a/solution.py
+++ b/solution.py
@@ -1,4 +1,3 @@
-import functools
 import jax
 import jax.numpy as jnp
 from jax import lax
@@ -21,6 +20,7 @@
 
 def greet():
     z, y, x = place()
+    i = lax.axis_index("ctx")
     barrier = pltpu.get_barrier_semaphore()
 
     def hello(device):
@@ -28,17 +28,20 @@
 
     hello(at(z, y, 1 - x))
     hello(at(z, 1 - y, x))
-
-    @pl.when(z > 0)
-    def _():
-        hello(at(z - 1, y, x))
-
-    @pl.when(z < 3)
-    def _():
-        hello(at(z + 1, y, x))
-
-    ends = (z == 0).astype(jnp.int32) + (z == 3).astype(jnp.int32)
-    pl.semaphore_wait(barrier, 4 - ends)
+    hello({"section": 1 - lax.axis_index("section")})
+    for there, device in (
+        (z > 0, at(z - 1, y, x)),
+        (z < 3, at(z + 1, y, x)),
+        (i > 0, {"ctx": i - 1}),
+        (i < 15, {"ctx": i + 1}),
+    ):
+
+        @pl.when(there)
+        def _():
+            hello(device)
+
+    ends = sum((c).astype(jnp.int32) for c in (z == 0, z == 3, i == 0, i == 15))
+    pl.semaphore_wait(barrier, 7 - ends)
 
 
 class Gather:
@@ -154,51 +157,263 @@
             self.each(t, body)
 
 
-def gather_kernel(conv, mix, conv_full, mix_full, send_sem, recv_sem, own_sem):
+PAD = 16
+LANES = 128
+TILE = 256
+
+
+class Halo:
+    def __init__(self, middle, halo, send_sem, recv_sem):
+        self.middle, self.halo = middle, halo
+        self.send_sem, self.recv_sem = send_sem, recv_sem
+        self.i = lax.axis_index("ctx")
+        self.rows = middle.shape[0]
+
+    def copy(self, slot):
+        first = self.rows - PAD if slot == 0 else 0
+        return pltpu.make_async_remote_copy(
+            src_ref=self.middle.at[pl.ds(first, PAD), :],
+            dst_ref=self.halo.at[slot],
+            send_sem=self.send_sem.at[slot],
+            recv_sem=self.recv_sem.at[slot],
+            device_id={"ctx": self.i + 1 if slot == 0 else self.i - 1},
+            device_id_type=MESH,
+        )
+
+    def sends(self, slot):
+        return self.i < 15 if slot == 0 else self.i > 0
+
+    def receives(self, slot):
+        return self.i > 0 if slot == 0 else self.i < 15
+
+    def start(self):
+        for slot in range(2):
+
+            @pl.when(self.sends(slot))
+            def _():
+                self.copy(slot).start()
+
+    def finish(self):
+        for slot in range(2):
+
+            @pl.when(self.receives(slot))
+            def _():
+                self.copy(slot).wait_recv()
+
+            @pl.when(jnp.logical_not(self.receives(slot)))
+            def _():
+                self.halo[slot] = jnp.zeros(self.halo.shape[1:], self.halo.dtype)
+
+            @pl.when(self.sends(slot))
+            def _():
+                self.copy(slot).wait_send()
+
+
+def columns(count, width, body):
+    def step(n, c):
+        body(pl.ds(pl.multiple_of(n * width, width), width), n)
+        return c
+
+    lax.fori_loop(0, count, step, 0)
+
+
+def windows(padded, halo, before, after, level):
+    rows, wide = before.shape
+
+    def body(cols, _):
+        padded[0:PAD, cols] = halo[0, :, cols].astype(jnp.float32)
+        padded[PAD + rows:2 * PAD + rows, cols] = halo[1, :, cols].astype(jnp.float32)
+        near = padded[PAD - 1:PAD - 1 + rows, cols]
+        far = padded[PAD - 2:PAD - 2 + rows, cols]
+        before[:, cols] = jnp.where(level == 0, near, far).astype(jnp.bfloat16)
+        near = padded[PAD + 1:PAD + 1 + rows, cols]
+        far = padded[PAD + 2:PAD + 2 + rows, cols]
+        after[:, cols] = jnp.where(level == 0, near, far).astype(jnp.bfloat16)
+
+    columns(wide // LANES, LANES, body)
+
+
+def across(left, right):
+    return lax.dot_general(left, right, (((1,), (1,)), ((), ())), preferred_element_type=jnp.float32)
+
+
+def tower_kernel(
+    conv_w, mix_w, inputs, scale, shift, cotangent, out,
+    conv_full, mix_full, padded, factor, low, mid, high, halo, total,
+    dpadded, dlow, dmid, dhigh, dhalo, dtotal, grad,
+    send_sem, recv_sem, own_sem, halo_send, halo_recv, dhalo_send, dhalo_recv, grad_send, grad_recv,
+):
+    level = lax.axis_index("section")
+    rows, wide = cotangent.shape
+    inner = total.shape[1]
+    plane = wide // 4
     greet()
-    gather = Gather(conv, mix, conv_full, mix_full, send_sem, recv_sem)
+    gather = Gather(conv_w, mix_w, conv_full, mix_full, send_sem, recv_sem)
     gather.hop(0, 0, 0)
     z, y, x = place()
     me = z * 4 + y * 2 + x
     local = [
         pltpu.make_async_copy(
-            conv.at[0],
+            conv_w.at[0],
             conv_full.at[:, pl.ds(pl.multiple_of(me * gather.depth, 16), gather.depth), :],
             own_sem.at[0],
         ),
         pltpu.make_async_copy(
-            mix.at[0],
+            mix_w.at[0],
             mix_full.at[pl.ds(pl.multiple_of(me * gather.inner, 16), gather.inner), :],
             own_sem.at[1],
         ),
     ]
     for copy in local:
         copy.start()
-    for t, ry, rx in HOPS[1:]:
-        gather.hop(t, ry, rx)
+
+    def front(cols, _):
+        gain = scale[:, cols]
+        pre = inputs[0, :, cols].astype(jnp.float32) * gain + shift[:, cols]
+        act, slope = gelu_parts(pre)
+        hidden = act.astype(jnp.bfloat16)
+        mid[:, cols] = hidden
+        padded[PAD:PAD + rows, cols] = hidden.astype(jnp.float32)
+        factor[:, cols] = slope * gain
+
+    columns(wide // LANES, LANES, front)
+
+    @pl.when(level == 1)
+    def _():
+        grad[...] = cotangent[...]
+
+    total[...] = jnp.zeros_like(total)
+    edges = Halo(mid, halo, halo_send, halo_recv)
+    edges.start()
     for copy in local:
         copy.wait()
+
+    def add_plane(t):
+        def body(sign):
+            off = pl.ds(pl.multiple_of((z + sign * t) * plane, plane), plane)
+
+            def tile(cols, _):
+                part = total[:, cols]
+                for k, window in enumerate((low, mid, high)):
+                    part += jnp.dot(window[:, off], conv_full[k, off, cols], preferred_element_type=jnp.float32)
+                total[:, cols] = part
+
+            columns(inner // TILE, TILE, tile)
+
+        gather.each(t, body)
+
+    for n, (t, ry, rx) in enumerate(HOPS[1:]):
+        gather.hop(t, ry, rx)
+        if n == 1:
+            edges.finish()
+            windows(padded, halo, low, high, level)
+        if ry and rx:
+            add_plane(t)
+
+    def slopes(cols, _):
+        total[:, cols] = gelu_parts(total[:, cols])[1]
+
+    columns(inner // LANES, LANES, slopes)
+
+    def hand(n):
+        cols = pl.ds(n * TILE, TILE)
+        return pltpu.make_async_remote_copy(
+            src_ref=out.at[0, :, cols],
+            dst_ref=grad.at[:, cols],
+            send_sem=grad_send.at[n],
+            recv_sem=grad_recv.at[n],
+            device_id={"section": 0},
+            device_id_type=MESH,
+        )
+
+    tiles = wide // TILE
+
+    @pl.when(level == 0)
+    def _():
+        for n in range(tiles):
+            hand_in = pltpu.make_async_remote_copy(
+                src_ref=out.at[0, :, pl.ds(n * TILE, TILE)],
+                dst_ref=grad.at[:, pl.ds(n * TILE, TILE)],
+                send_sem=grad_send.at[n],
+                recv_sem=grad_recv.at[n],
+                device_id={"section": 1},
+                device_id_type=MESH,
+            )
+            hand_in.wait_recv()
+
+    def back(cols, n):
+        value = across(grad[...], mix_full[cols, :]) * total[:, cols]
+        dconv = value.astype(jnp.bfloat16)
+        dmid[:, cols] = dconv
+        dpadded[PAD:PAD + rows, cols] = dconv.astype(jnp.float32)
+
+    columns(inner // TILE, TILE, back)
+    dedges = Halo(dmid, dhalo, dhalo_send, dhalo_recv)
+    dedges.start()
+
+    def middle(cols, n):
+        dtotal[:, cols] = across(dmid[...], conv_full[1, cols, :])
+
+    columns(tiles, TILE, middle)
+    dedges.finish()
+    windows(dpadded, dhalo, dlow, dhigh, level)
+    for n in range(tiles):
+        cols = pl.ds(n * TILE, TILE)
+        dhidden = dtotal[:, cols] + across(dhigh[...], conv_full[0, cols, :]) + across(dlow[...], conv_full[2, cols, :])
+        out[0, :, cols] = (grad[:, cols].astype(jnp.float32) + dhidden * factor[:, cols]).astype(jnp.bfloat16)
+
+        @pl.when(level == 1)
+        def _():
+            hand(n).start()
+
+    @pl.when(level == 1)
+    def _():
+        for n in range(tiles):
+            hand(n).wait_send()
+
     gather.drain()
 
 
-def gathered(conv, mix):
-    count = lax.axis_size("ctx")
-    any_space = pl.BlockSpec(memory_space=pl.ANY)
+def tower(layer_inputs, conv_weight, mix_weight, bn_scale, bn_shift, cotangent):
+    rows, wide = cotangent.shape
+    inner = conv_weight.shape[3]
+    anywhere = pl.BlockSpec(memory_space=pl.ANY)
+    vmem = pl.BlockSpec(memory_space=pltpu.VMEM)
+    bf16, f32 = jnp.bfloat16, jnp.float32
     return pl.pallas_call(
-        gather_kernel,
-        out_shape=(
-            jax.ShapeDtypeStruct((3, count * conv.shape[2], conv.shape[3]), conv.dtype),
-            jax.ShapeDtypeStruct((count * mix.shape[1], mix.shape[2]), mix.dtype),
-        ),
-        in_specs=[any_space] * 2,
-        out_specs=(any_space, any_space),
+        tower_kernel,
+        out_shape=jax.ShapeDtypeStruct(layer_inputs.shape, bf16),
+        in_specs=[anywhere, anywhere, vmem, vmem, vmem, vmem],
+        out_specs=vmem,
         scratch_shapes=[
+            pltpu.VMEM((3, wide, inner), bf16),
+            pltpu.VMEM((inner, wide), bf16),
+            pltpu.VMEM((rows + 2 * PAD, wide), f32),
+            pltpu.VMEM((rows, wide), f32),
+            pltpu.VMEM((rows, wide), bf16),
+            pltpu.VMEM((rows, wide), bf16),
+            pltpu.VMEM((rows, wide), bf16),
+            pltpu.VMEM((2, PAD, wide), bf16),
+            pltpu.VMEM((rows, inner), f32),
+            pltpu.VMEM((rows + 2 * PAD, inner), f32),
+            pltpu.VMEM((rows, inner), bf16),
+            pltpu.VMEM((rows, inner), bf16),
+            pltpu.VMEM((rows, inner), bf16),
+            pltpu.VMEM((2, PAD, inner), bf16),
+            pltpu.VMEM((rows, wide), f32),
+            pltpu.VMEM((rows, wide), bf16),
             pltpu.SemaphoreType.DMA((4, 16, 4, 2)),
             pltpu.SemaphoreType.DMA((4, 16, 2)),
             pltpu.SemaphoreType.DMA((2,)),
+            pltpu.SemaphoreType.DMA((2,)),
+            pltpu.SemaphoreType.DMA((2,)),
+            pltpu.SemaphoreType.DMA((2,)),
+            pltpu.SemaphoreType.DMA((2,)),
+            pltpu.SemaphoreType.DMA((wide // TILE,)),
+            pltpu.SemaphoreType.DMA((wide // TILE,)),
         ],
         compiler_params=pltpu.CompilerParams(collective_id=0, has_side_effects=True),
-    )(conv, mix)
+    )(conv_weight, mix_weight, layer_inputs, bn_scale, bn_shift, cotangent)
 
 
 def extended(cells, sides, width):
@@ -234,11 +449,10 @@
     sections = lax.axis_size("section")
     level = lax.axis_index("section")
     widest = 2 ** (sections - 1)
-    if lax.axis_size("ctx") == 16:
-        conv_full, mix_full = gathered(conv_weight, mix_weight)
-    else:
-        conv_full = lax.all_gather(conv_weight, "ctx", axis=2, tiled=True)[0]
-        mix_full = lax.all_gather(mix_weight, "ctx", axis=1, tiled=True)[0]
+    if lax.axis_size("ctx") == 16 and sections == 2:
+        return tower(layer_inputs, conv_weight, mix_weight, bn_scale, bn_shift, cotangent)
+    conv_full = lax.all_gather(conv_weight, "ctx", axis=2, tiled=True)[0]
+    mix_full = lax.all_gather(mix_weight, "ctx", axis=1, tiled=True)[0]
     rows = cotangent.shape[0]
     inner = mix_full.shape[0]
     spacing = jnp.left_shift(jnp.int32(1), level)

time: 145 us -> 105 us (0.72)
  the two profiles are of different devices: /device:TPU:9 before, /device:TPU:0 now
where the time goes in v2:
time: 105 us
  Pallas kernels  103 us (98%)
  local copies, waits for them, and re-layouts  2.06 us (2%)
    pallas_call x1, Pallas kernels, tower(): pl.pallas_call(tower_kernel, out_shape=jax.ShapeDtypeStruct(layer_inputs....  103 us

profile of v2, /device:TPU:0, one launch (start us, length us, event | category | flops | bytes accessed | tf_op | source)
XLA Modules:
  0.0 104.7 jit_solution(12958546912471632926)
XLA Ops:
  0.0 102.6 %shard_map.64 = bf16[1,256,1536]{2,1,0:T(8,128)(2,1)} custom-call(bf16[1,3,96,768]{3,2,1,0:T(8,128)(2,1)} %conv_w.1, bf16[1,48,1536]{2,1,0:T(8,128)(2,1)} %mix_w.1, bf16[1,256,1536]{2,1,0:T(8,128)(2,1)} %inputs.1, f32[1,1536]{1,0:T(1,128)} %scale.1, f32[1,1536]{1,0:T(1,128)} %shift.1, bf16[256,1536]{1,0:T(8,128)(2,1)} %cotangent.1), custom_call_target="tpu_custom_call" | custom-call | tf_op jit(solution)/shard_map/pallas_call | solution.py:383
  102.6 2.1 %copy.8 = bf16[1,256,1536]{2,1,0:T(8,128)(2,1)} copy(bf16[1,256,1536]{2,1,0:T(8,128)(2,1)} %shard_map.64) | data formatting | bytes 1572864

commit v3 on v2

--- a/solution.py
+++ b/solution.py
@@ -160,6 +160,7 @@
 PAD = 16
 LANES = 128
 TILE = 256
+LEAD = 5
 
 
 class Halo:
@@ -241,7 +242,7 @@
     conv_w, mix_w, inputs, scale, shift, cotangent, out,
     conv_full, mix_full, padded, factor, low, mid, high, halo, total,
     dpadded, dlow, dmid, dhigh, dhalo, dtotal, grad,
-    send_sem, recv_sem, own_sem, halo_send, halo_recv, dhalo_send, dhalo_recv, grad_send, grad_recv,
+    send_sem, recv_sem, own_sem, halo_send, halo_recv, dhalo_send, dhalo_recv, grad_send, grad_recv, gate,
 ):
     level = lax.axis_index("section")
     rows, wide = cotangent.shape
@@ -249,7 +250,11 @@
     plane = wide // 4
     greet()
     gather = Gather(conv_w, mix_w, conv_full, mix_full, send_sem, recv_sem)
-    gather.hop(0, 0, 0)
+
+    @pl.when(level == 1)
+    def _():
+        gather.hop(0, 0, 0)
+
     z, y, x = place()
     me = z * 4 + y * 2 + x
     local = [
@@ -288,6 +293,11 @@
     for copy in local:
         copy.wait()
 
+    @pl.when(level == 0)
+    def _():
+        pl.semaphore_wait(gate, 1)
+        gather.hop(0, 0, 0)
+
     def add_plane(t):
         def body(sign):
             off = pl.ds(pl.multiple_of((z + sign * t) * plane, plane), plane)
@@ -304,6 +314,12 @@
 
     for n, (t, ry, rx) in enumerate(HOPS[1:]):
         gather.hop(t, ry, rx)
+        if n == LEAD:
+
+            @pl.when(level == 1)
+            def _():
+                pl.semaphore_signal(gate, inc=1, device_id={"section": 0}, device_id_type=MESH)
+
         if n == 1:
             edges.finish()
             windows(padded, halo, low, high, level)
@@ -411,6 +427,7 @@
             pltpu.SemaphoreType.DMA((2,)),
             pltpu.SemaphoreType.DMA((wide // TILE,)),
             pltpu.SemaphoreType.DMA((wide // TILE,)),
+            pltpu.SemaphoreType.REGULAR,
         ],
         compiler_params=pltpu.CompilerParams(collective_id=0, has_side_effects=True),
     )(conv_weight, mix_weight, layer_inputs, bn_scale, bn_shift, cotangent)

time: 105 us -> 105 us (level)
  no operation moved by 1% of the time
where the time goes in v3:
time: 105 us
  Pallas kernels  103 us (98%)
  local copies, waits for them, and re-layouts  2.06 us (2%)
    pallas_call x1, Pallas kernels, tower(): pl.pallas_call(tower_kernel, out_shape=jax.ShapeDtypeStruct(layer_inputs....  103 us

profile of v3, /device:TPU:0, one launch (start us, length us, event | category | flops | bytes accessed | tf_op | source)
XLA Modules:
  0.0 105.0 jit_solution(10325192541462508894)
XLA Ops:
  0.0 102.9 %shard_map.64 = bf16[1,256,1536]{2,1,0:T(8,128)(2,1)} custom-call(bf16[1,3,96,768]{3,2,1,0:T(8,128)(2,1)} %conv_w.1, bf16[1,48,1536]{2,1,0:T(8,128)(2,1)} %mix_w.1, bf16[1,256,1536]{2,1,0:T(8,128)(2,1)} %inputs.1, f32[1,1536]{1,0:T(1,128)} %scale.1, f32[1,1536]{1,0:T(1,128)} %shift.1, bf16[256,1536]{1,0:T(8,128)(2,1)} %cotangent.1), custom_call_target="tpu_custom_call" | custom-call | tf_op jit(solution)/shard_map/pallas_call | solution.py:399
  102.9 2.1 %copy.8 = bf16[1,256,1536]{2,1,0:T(8,128)(2,1)} copy(bf16[1,256,1536]{2,1,0:T(8,128)(2,1)} %shard_map.64) | data formatting | bytes 1572864

commit v4 on v3

--- a/solution.py
+++ b/solution.py
@@ -160,7 +160,7 @@
 PAD = 16
 LANES = 128
 TILE = 256
-LEAD = 5
+LEAD = 2
 
 
 class Halo:

time: 105 us -> 104 us (level)
  Pallas kernels: 103 us -> 101 us
    pallas_call x1, Pallas kernels: 103 us -> 101 us  [tower(): pl.pallas_call(tower_kernel, out_shape=jax.ShapeDtypeStruct(layer_inputs....]
where the time goes in v4:
time: 104 us; the launch traced here: 103 us
  Pallas kernels  101 us (97%)
  local copies, waits for them, and re-layouts  2.06 us (2%)
    pallas_call x1, Pallas kernels, tower(): pl.pallas_call(tower_kernel, out_shape=jax.ShapeDtypeStruct(layer_inputs....  101 us

profile of v4, /device:TPU:0, one launch (start us, length us, event | category | flops | bytes accessed | tf_op | source)
XLA Modules:
  0.0 103.5 jit_solution(3717211439317910634)
XLA Ops:
  0.0 101.4 %shard_map.64 = bf16[1,256,1536]{2,1,0:T(8,128)(2,1)} custom-call(bf16[1,3,96,768]{3,2,1,0:T(8,128)(2,1)} %conv_w.1, bf16[1,48,1536]{2,1,0:T(8,128)(2,1)} %mix_w.1, bf16[1,256,1536]{2,1,0:T(8,128)(2,1)} %inputs.1, f32[1,1536]{1,0:T(1,128)} %scale.1, f32[1,1536]{1,0:T(1,128)} %shift.1, bf16[256,1536]{1,0:T(8,128)(2,1)} %cotangent.1), custom_call_target="tpu_custom_call" | custom-call | tf_op jit(solution)/shard_map/pallas_call | solution.py:399
  101.4 2.1 %copy.8 = bf16[1,256,1536]{2,1,0:T(8,128)(2,1)} copy(bf16[1,256,1536]{2,1,0:T(8,128)(2,1)} %shard_map.64) | data formatting | bytes 1572864

commit v5 on v4

--- a/solution.py
+++ b/solution.py
@@ -87,13 +87,13 @@
             for m in range(2)
         ]
 
-    def visit(self, t, ry, rx, part, sign, act):
+    def visit(self, t, ry, rx, part, sign, act, legs=(0, 1, 2)):
         z, y, x = place()
         source = (z + sign * t) * 4 + (1 - y if ry else y) * 2 + (1 - x if rx else x)
         mine = not (t or ry or rx)
         differs = {"x": rx, "y": ry, "z": t}
         order = self.parts[part][0]
-        for n in (2, 1, 0):
+        for n in legs:
             axis = order[n]
             if any(differs[later] for later in order[n + 1:]):
                 continue
@@ -138,11 +138,15 @@
         for copy in self.copies(part, source, False, 0, at(z, y, 1 - x)):
             copy.wait_recv()
 
+    def begin(self):
+        for leg in range(3):
+            for part in range(4):
+                self.visit(0, 0, 0, part, 0, lambda cs: [c.start() for c in cs], (leg,))
+
     def hop(self, t, ry, rx):
         def body(sign):
             for part in range(4):
-                if t or ry or rx:
-                    self.arrive(t, ry, rx, part, sign)
+                self.arrive(t, ry, rx, part, sign)
                 self.visit(t, ry, rx, part, sign, lambda cs: [c.start() for c in cs])
 
         self.each(t, body)
@@ -253,7 +257,7 @@
 
     @pl.when(level == 1)
     def _():
-        gather.hop(0, 0, 0)
+        gather.begin()
 
     z, y, x = place()
     me = z * 4 + y * 2 + x
@@ -296,7 +300,7 @@
     @pl.when(level == 0)
     def _():
         pl.semaphore_wait(gate, 1)
-        gather.hop(0, 0, 0)
+        gather.begin()
 
     def add_plane(t):
         def body(sign):

time: 104 us -> 103 us (level)
  no operation moved by 1% of the time
where the time goes in v5:
time: 103 us
  Pallas kernels  101 us (98%)
  local copies, waits for them, and re-layouts  2.06 us (2%)
    pallas_call x1, Pallas kernels, tower(): pl.pallas_call(tower_kernel, out_shape=jax.ShapeDtypeStruct(layer_inputs....  101 us
    unnamed x1, local copies, waits for them, and re-layouts  2.06 us

profile of v5, /device:TPU:0, one launch (start us, length us, event | category | flops | bytes accessed | tf_op | source)
XLA Modules:
  0.0 103.3 jit_solution(8076797987974388964)
XLA Ops:
  0.0 101.2 %shard_map.64 = bf16[1,256,1536]{2,1,0:T(8,128)(2,1)} custom-call(bf16[1,3,96,768]{3,2,1,0:T(8,128)(2,1)} %conv_w.1, bf16[1,48,1536]{2,1,0:T(8,128)(2,1)} %mix_w.1, bf16[1,256,1536]{2,1,0:T(8,128)(2,1)} %inputs.1, f32[1,1536]{1,0:T(1,128)} %scale.1, f32[1,1536]{1,0:T(1,128)} %shift.1, bf16[256,1536]{1,0:T(8,128)(2,1)} %cotangent.1), custom_call_target="tpu_custom_call" | custom-call | tf_op jit(solution)/shard_map/pallas_call | solution.py:403
  101.3 2.1 %copy.8 = bf16[1,256,1536]{2,1,0:T(8,128)(2,1)} copy(bf16[1,256,1536]{2,1,0:T(8,128)(2,1)} %shard_map.64) | data formatting | bytes 1572864
